TPU v7x, 128 devices: a whole 4x4x4 slice. The times are simulated.
128 devices in a mesh: group: 8 (over y, core), member: 16 (over z, x).
Axes of the slice: x: 4, y: 4, z: 4, core: 2. Of those that a mesh axis runs over, the one named last changes fastest.
Arguments:
- hidden: bfloat16 [49152, 3584], P(('group', 'member')), may hold values from -30 to 30
- projection: bfloat16 [3584, 1024], replicated, may hold values from -0.09375 to 0.09375
- inv_temp: float32 [1], replicated, may hold values from 10 to 80
- partners: int32 [128, 12], P(('group', 'member')), may hold values from 0 to 127, as said below
- positives: int32 [49152], P(('group', 'member')), may hold values from 0 to 49151, as said below
Outputs:
- loss: float32 [], replicated
- grad_hidden: bfloat16 [49152, 3584], P(('group', 'member'))
- grad_proj: float32 [3584, 1024], P(('group', 'member'))
Inputs may be any that keep to these rules, and one draw needn't show every extreme that they name: Block ids are numbered in row order. partners[b] are 12 distinct blocks of b's own group of 16 consecutive blocks, none equal to b; within a group they are b's index in the group XORed with 12 distinct nonzero offsets common to that group, so b lists c exactly when c lists b. positives pairs the rows of each block among themselves: positives_i lies in i's block, differs from i, and positives of positives_i is i.
All inputs are finite; a program needn't handle non-finite values.
Results may differ from a plain program's by a relative error of at most 0.006.
Values may be sent and summed in bfloat16 or wider, within the bound.
No kernel may reach another device: no remote copies, remote signals or barrier semaphores. Data moves between devices by JAX's collectives and lax.ppermute only.
A program may use at most 128 MiB of HBM per device.

v0:
```python
import jax
import jax.numpy as jnp
from jax import lax
from jax.sharding import PartitionSpec as P

epsilon = 1e-06


def per_device(hidden, projection, inv_temp, partners, positives):
    rows = hidden.shape[0]
    width = projection.shape[1]
    members = lax.axis_size("member")
    groups = lax.axis_size("group")
    mine = lax.axis_index("member")
    projected = jnp.dot(hidden, projection, preferred_element_type=jnp.float32)
    lengths = jnp.sqrt(jnp.sum(projected * projected, axis=1, keepdims=True) + epsilon)
    unit_rows = projected / lengths
    unit_low = unit_rows.astype(jnp.bfloat16)
    gathered = lax.all_gather(unit_low, "member", axis=0, tiled=True).reshape(members, rows, width)
    chosen = jnp.concatenate([mine[None], partners[0] % members])
    others = gathered[chosen]
    scale = inv_temp[0]
    tiles_count = partners.shape[1] + 1
    first = (jnp.arange(tiles_count) == 0)[:, None, None]
    columns = jnp.arange(rows)
    self_mask = first & (columns[:, None] == columns[None, :])[None]
    scores = scale * jnp.einsum("id,pjd->pij", unit_low, others, preferred_element_type=jnp.float32)
    scores = jnp.where(self_mask, -jnp.inf, scores)
    highest = jnp.max(scores, axis=(0, 2))
    log_totals = highest + jnp.log(jnp.sum(jnp.exp(scores - highest[None, :, None]), axis=(0, 2)))
    local_pos = positives % rows
    target = first & (columns[None, None, :] == local_pos[:, None][None])
    pos_scores = jnp.sum(jnp.where(target, scores, 0.0), axis=(0, 2))
    total = lax.psum(jnp.sum(log_totals - pos_scores), ("group", "member"))
    loss = total / (groups * members * rows)
    all_totals = lax.all_gather(log_totals, "member", axis=0, tiled=True).reshape(members, rows)
    row_prob = jnp.exp(scores - log_totals[None, :, None])
    col_prob = jnp.exp(scores - all_totals[chosen][:, None, :])
    weights = (row_prob + col_prob - 2.0 * target).astype(jnp.bfloat16)
    grad_unit = scale * jnp.einsum(
        "pij,pjd->id", weights, others, preferred_element_type=jnp.float32
    )
    along = jnp.sum(unit_rows * grad_unit, axis=1, keepdims=True)
    grad_projected = ((grad_unit - unit_rows * along) / lengths).astype(jnp.bfloat16)
    grad_hidden = lax.dot_general(
        grad_projected, projection, (((1,), (1,)), ((), ())), preferred_element_type=jnp.float32
    ).astype(jnp.bfloat16)
    grad_proj = lax.psum_scatter(
        lax.dot_general(
            hidden, grad_projected, (((0,), (0,)), ((), ())), preferred_element_type=jnp.float32
        ),
        ("group", "member"),
        scatter_dimension=0,
        tiled=True,
    )
    return (loss, grad_hidden, grad_proj)


def solution(mesh):
    return jax.shard_map(
        per_device,
        mesh=mesh,
        in_specs=(
            P(("group", "member"), None),
            P(),
            P(),
            P(("group", "member"), None),
            P(("group", "member")),
        ),
        out_specs=(P(), P(("group", "member"), None), P(("group", "member"), None)),
        check_vma=False,
    )
```

profile of v0, /device:TPU:1, one launch (start us, length us, event | category | flops | bytes accessed | tf_op | source)
XLA Modules:
  0.0 362.2 jit_solution(9420817212567875197)
XLA Ops:
  7.2 0.0 copy-start
  7.2 0.0 copy-start.11
  7.2 0.0 copy-start.10
  7.2 0.0 all-gather.3.cloned.1.call-start
  7.2 1.7 copy-done
  8.9 5.4 %multiply_reduce_fusion.1 = (f32[384]{0:T(512)S(1)}, f32[384,1024]{1,0:T(8,128)S(1)}) fusion(bf16[384,3584]{1,0:T(8,128)(2,1)S(1)} %copy-done, bf16[3584,1024]{1,0:T(8,128)(2,1)} %param.6), kind=kOutput, calls=%fused_computation.22 | convolution fusion | flops 2819358208 | bytes 11666944 | tf_op jit(solution)/shard_map/dot_general | solution.py:15
  14.3 0.0 copy-start.2
  14.4 1.2 copy-done.2
  15.5 1.1 fusion.22
  16.6 0.0 all-gather.3.cloned.1.call-update
  16.7 0.0 all-reduce.3.cloned.1.call-start
  17.4 0.0 copy-done.11
  17.4 0.1 fusion.18
  17.5 0.7 iota_compare_fusion.1
  18.2 0.0 copy-done.10
  18.2 0.7 iota_compare_fusion
  19.0 91.2 %all-gather.3.cloned.1.call-done = bf16[6144,1024]{1,0:T(8,128)(2,1)} async-done(((bf16[384,1024]{1,0:T(8,128)(2,1)}), bf16[6144,1024]{1,0:T(8,128)(2,1)}) %all-gather.3.cloned.1.call-update) | async-done | bytes 12582928 | tf_op jit(solution)/shard_map/all_gather | solution.py:19
  110.2 0.0 copy-start.4
  110.2 10.4 %gather_fusion = bf16[13,384,1024]{2,1,0:T(8,128)(2,1)} fusion(bf16[16,384,1024]{2,1,0:T(8,128)(2,1)} %bitcast.47, s32[1024]{0:T(1024)S(1)} %pad_clamp_fusion), kind=kCustom, calls=%fused_computation | custom fusion | bytes 20447284 | tf_op jit(solution)/shard_map/gather | solution.py:21
  120.5 0.0 copy-done.4
  120.5 0.0 copy-start.6
  120.5 0.0 copy-start.8
  120.5 10.0 %fusion.11 = (f32[384]{0:T(512)S(1)}, f32[13,384,384]{2,1,0:T(8,128)S(1)}) fusion(f32[]{:T(128)} %bitcast.44, pred[384,384]{0,1:T(8,128)(4,1)} %iota_compare_fusion.1, pred[13]{0:T(512)(128)(4,1)S(1)} %iota_compare_fusion.2, bf16[13,384,1024]{2,1,0:T(8,128)(2,1)} %gather_fusion, bf16[384,1024]{1,0:T(8,128)(2,1)S(1)} %copy-done.4), kind=kOutput, calls=%fused_computation.18 | convolution fusion | flops 3933535744 | bytes 18826768 | tf_op jit(solution)/shard_map/id,pjd->pij/dot_general | solution.py:27
  130.5 0.0 copy-start.1
  130.5 0.0 copy-done.6
  130.5 0.0 copy-done.8
  130.5 0.0 copy-start.7
  130.5 0.0 copy-start.9
  130.6 3.2 fusion
  133.7 0.0 copy-done.1
  133.8 0.6 subtract_reduce_fusion
  134.4 17.7 %all-gather = f32[16,1,384]{2,1,0:T(1,128)S(1)} all-gather(f32[1,1,384]{2,1,0:T(1,128)S(1)} %reshape.161), channel_id=1, replica_groups=mesh['group'=8,'member'=16] {'member'}, dimensions={0}, use_global_device_ids=true | all-gather | bytes 26112 | tf_op jit(solution)/shard_map/all_gather | solution.py:36
  152.1 0.6 gather_fusion.1
  152.7 0.0 copy-done.7
  152.7 0.0 copy-done.9
  152.7 0.0 copy-start.3
  152.7 12.8 %multiply_reduce_fusion = (f32[384]{0:T(512)S(1)}, f32[384,1024]{1,0:T(8,128)S(1)}) fusion(f32[384,1024]{1,0:T(8,128)} %copy-done.2, f32[384]{0:T(512)S(1)} %add_sqrt_fusion, bf16[13,384,1024]{2,1,0:T(8,128)(2,1)} %gather_fusion, f32[13,384]{1,0:T(8,128)S(1)} %gather_fusion.1, f32[384]{0:T(512)S(1)} %get-tuple-element.12, ...), kind=kOutput, calls=%fused_computation.21 | convolution fusion | flops 3946610176 | bytes 21356560 | tf_op jit(solution)/shard_map/pij,pjd->id/dot_general | solution.py:40
  165.5 0.0 copy-start.5
  165.5 1.1 copy-done.5
  166.6 0.0 copy-done.3
  166.6 7.5 %convolution_bitcast_fusion = f32[3584,1024]{0,1:T(8,128)} fusion(bf16[384,3584]{1,0:T(8,128)(2,1)S(1)} %copy-done, f32[384,1024]{1,0:T(8,128)S(1)} %get-tuple-element.18, f32[384]{0:T(512)S(1)} %get-tuple-element.17, f32[384]{0:T(512)S(1)} %add_sqrt_fusion, f32[384,1024]{1,0:T(8,128)S(1)} %copy-done.3), kind=kOutput, calls=%fused_computation.4 | convolution fusion | flops 2820538368 | bytes 20581376 | tf_op jit(solution)/shard_map/dot_general | solution.py:49
  174.2 0.0 all-reduce.3.cloned.1.call-update
  174.2 69.1 %psum.7 = f32[]{:T(128)} all-reduce(f32[]{:T(128)} %get-tuple-element.11), channel_id=1, replica_groups=mesh['group'=8,'member'=16] {'group','member'}, use_global_device_ids=true, to_apply=%region_5.6 | all-reduce | flops 1 | bytes 8 | tf_op jit(solution)/shard_map/psum | solution.py:34
  243.9 8.8 %convolution_convert_fusion = bf16[384,3584]{1,0:T(8,128)(2,1)} fusion(bf16[3584,1024]{1,0:T(8,128)(2,1)} %param.6, f32[384,1024]{1,0:T(8,128)} %copy-done.5, f32[384]{0:T(512)S(1)} %get-tuple-element.17, f32[384]{0:T(512)S(1)} %add_sqrt_fusion, f32[384,1024]{1,0:T(8,128)} %copy-done.2), kind=kOutput, calls=%fused_computation.10 | convolution fusion | flops 2821914624 | bytes 13241344 | tf_op jit(solution)/shard_map/dot_general | solution.py:45
  252.7 99.2 %all-reduce.3.cloned.1.call-done = f32[3584,1024]{0,1:T(8,128)} async-done(((f32[3584,1024]{0,1:T(8,128)}), f32[3584,1024]{0,1:T(8,128)}) %all-reduce.3.cloned.1.call-update) | async-done | bytes 14680080
  352.0 1.4 constant_dynamic-slice_fusion
  353.4 0.9 copy.11
  (7 shorter events, 0.0 us)
Async XLA Ops:
  7.2 1.8 copy-start
  7.2 10.2 %copy-start.11 = (s32[1,12]{1,0:T(1,128)S(1)}, s32[1,12]{1,0:T(1,128)}, u32[]{:S(2)}) copy-start(s32[1,12]{1,0:T(1,128)} %param.8) | copy-start | bytes 148
  7.2 11.0 %copy-start.10 = (s32[384]{0:T(512)S(1)}, s32[384]{0:T(512)}, u32[]{:S(2)}) copy-start(s32[384]{0:T(512)} %param.9) | copy-start | bytes 4612
  7.2 103.0 %all-gather.3.cloned.1.call-start = ((), (), s32[]{:S(2)}) async-start(), calls=%async_computation | async-start | bytes 13369344 | tf_op jit(solution)/shard_map/all_gather | solution.py:19
  14.3 1.2 copy-start.2
  16.7 335.3 %all-reduce.3.cloned.1.call-start = ((), (), s32[]{:S(2)}) async-start(), calls=%async_computation.1 | async-start | bytes 29360128
  110.2 10.4 %copy-start.4 = (bf16[384,1024]{1,0:T(8,128)(2,1)S(1)}, bf16[384,1024]{1,0:T(8,128)(2,1)}, u32[]{:S(2)}) copy-start(bf16[384,1024]{1,0:T(8,128)(2,1)} %fusion.22) | copy-start | bytes 2359300
  120.5 10.0 %copy-start.6 = (pred[384,384]{0,1:T(8,128)(4,1)S(1)}, pred[384,384]{0,1:T(8,128)(4,1)}, u32[]{:S(2)}) copy-start(pred[384,384]{0,1:T(8,128)(4,1)} %iota_compare_fusion.1) | copy-start | bytes 442372
  120.5 10.0 %copy-start.8 = (pred[384,384]{0,1:T(8,128)(4,1)S(1)}, pred[384,384]{0,1:T(8,128)(4,1)}, u32[]{:S(2)}) copy-start(pred[384,384]{0,1:T(8,128)(4,1)} %iota_compare_fusion) | copy-start | bytes 442372
  130.5 3.2 copy-start.1
  130.5 22.1 %copy-start.7 = (pred[384,384]{0,1:T(8,128)(4,1)S(1)}, pred[384,384]{0,1:T(8,128)(4,1)}, u32[]{:S(2)}) copy-start(pred[384,384]{0,1:T(8,128)(4,1)} %iota_compare_fusion.1) | copy-start | bytes 442372
  130.5 22.1 %copy-start.9 = (pred[384,384]{0,1:T(8,128)(4,1)S(1)}, pred[384,384]{0,1:T(8,128)(4,1)}, u32[]{:S(2)}) copy-start(pred[384,384]{0,1:T(8,128)(4,1)} %iota_compare_fusion) | copy-start | bytes 442372
  152.7 13.9 %copy-start.3 = (f32[384,1024]{1,0:T(8,128)S(1)}, f32[384,1024]{1,0:T(8,128)}, u32[]{:S(2)}) copy-start(f32[384,1024]{1,0:T(8,128)} %copy-done.2) | copy-start | bytes 4718596
  165.5 1.1 copy-start.5
Sparse Core Ops, SparseCore 0:
  16.8 93.3 all-gather.2
  174.3 177.6 all-reduce.2
where the time goes:
time: 362 us
  waiting for transfers between devices  190 us (52%)
  blocking collectives  86.8 us (24%)
  matrix products  44.5 us (12%)
  local copies, waits for them, and re-layouts  17.3 us (5%)
  between operations  16.6 us (5%)
  other arithmetic  6.46 us (2%)
    unnamed x3, waiting for transfers between devices  99.2 us
    all_gather x1, waiting for transfers between devices, per_device(): lax.all_gather(unit_low, 'member', axis=0, tiled=True)  91.2 us
    psum x1, blocking collectives, per_device(): total = lax.psum(jnp.sum(log_totals - pos_scores), ('group', 'member'))  69.1 us
    all_gather x1, blocking collectives, per_device(): lax.all_gather(log_totals, 'member', axis=0, tiled=True)  17.7 us
    dot_general x1, matrix products, per_device(): jnp.einsum('pij,pjd->id', weights, others, preferred_element_type=jnp.flo...  12.8 us
    gather x1, local copies, waits for them, and re-layouts, per_device(): others = gathered[chosen]  10.4 us
    dot_general x1, matrix products, per_device(): jnp.einsum('id,pjd->pij', unit_low, others, preferred_element_type=jnp.fl...  9.95 us
    dot_general x1, matrix products, per_device(): lax.dot_general(grad_projected, projection, (((1,), (1,)), ((), ())), pre...  8.83 us
  transfers between devices with their start and end apart: 2, of which 2 were waited for; matrix products, arithmetic and copies ran while one was open for 3% of the time, Pallas kernels for 0%

commit v1 on v0

--- a/solution.py
+++ b/solution.py
@@ -4,6 +4,12 @@
 from jax.sharding import PartitionSpec as P
 
 epsilon = 1e-06
+
+
+def pair_the_inputs(array_in, bus_axis):
+    current_arr = jnp.stack([array_in for _ in range(lax.axis_size(bus_axis))], axis=0)
+    k_now = lax.all_to_all(current_arr, bus_axis, 0, 0)
+    return jnp.concatenate(k_now, axis=0)
 
 
 def per_device(hidden, projection, inv_temp, partners, positives):
@@ -16,7 +22,7 @@
     lengths = jnp.sqrt(jnp.sum(projected * projected, axis=1, keepdims=True) + epsilon)
     unit_rows = projected / lengths
     unit_low = unit_rows.astype(jnp.bfloat16)
-    gathered = lax.all_gather(unit_low, "member", axis=0, tiled=True).reshape(members, rows, width)
+    gathered = pair_the_inputs(unit_low, "member").reshape(members, rows, width)
     chosen = jnp.concatenate([mine[None], partners[0] % members])
     others = gathered[chosen]
     scale = inv_temp[0]

time: 362 us -> 472 us (1.30)
  waiting for transfers between devices: 190 us -> 282 us
  local copies, waits for them, and re-layouts: 17.3 us -> 26.4 us
  starting transfers between devices: 0.08 us -> 8.65 us
    all_to_all x0 -> x1, waiting for transfers between devices: none -> 184 us  [pair_the_inputs(): k_now = lax.all_to_all(current_arr, bus_axis, 0, 0)]
    all_gather x1 -> x0, waiting for transfers between devices: 91.2 us -> none  [per_device(): lax.all_gather(unit_low, 'member', axis=0, tiled=True)]
    all_to_all x0 -> x1, starting transfers between devices: none -> 8.6 us  [pair_the_inputs(): k_now = lax.all_to_all(current_arr, bus_axis, 0, 0)]
    another operation x0 -> x1, local copies, waits for them, and re-layouts: none -> 6.09 us  [pair_the_inputs(): jnp.stack([array_in for _ in range(lax.axis_size(bus_axis))], axis=0)]
    unnamed x3 -> x2, waiting for transfers between devices: 99.2 us -> 98.5 us
  transfers between devices with their start and end apart: 2 -> 2, of which waited for: 2 -> 2; matrix products, arithmetic and copies ran while one was open for 3% -> 2% of each run, Pallas kernels for 0% -> 0%
where the time goes in v1:
time: 472 us; the launch traced here: 471 us
  waiting for transfers between devices  282 us (60%)
  blocking collectives  87.7 us (19%)
  matrix products  44.4 us (9%)
  local copies, waits for them, and re-layouts  26.4 us (6%)
  between operations  16.6 us (4%)
  starting transfers between devices  8.65 us (2%)
  other arithmetic  5.58 us (1%)
    all_to_all x1, waiting for transfers between devices, pair_the_inputs(): k_now = lax.all_to_all(current_arr, bus_axis, 0, 0)  184 us
    unnamed x2, waiting for transfers between devices  98.5 us
    psum x1, blocking collectives, per_device(): total = lax.psum(jnp.sum(log_totals - pos_scores), ('group', 'member'))  71.4 us
    all_gather x1, blocking collectives, per_device(): lax.all_gather(log_totals, 'member', axis=0, tiled=True)  16.3 us
    dot_general x1, matrix products, per_device(): jnp.einsum('pij,pjd->id', weights, others, preferred_element_type=jnp.flo...  12.8 us
    gather x1, local copies, waits for them, and re-layouts, per_device(): others = gathered[chosen]  10.3 us
    dot_general x1, matrix products, per_device(): jnp.einsum('id,pjd->pij', unit_low, others, preferred_element_type=jnp.fl...  9.91 us
  transfers between devices with their start and end apart: 2, of which 2 were waited for; matrix products, arithmetic and copies ran while one was open for 2% of the time, Pallas kernels for 0%

profile of v1, /device:TPU:1, one launch (start us, length us, event | category | flops | bytes accessed | tf_op | source)
XLA Modules:
  0.0 471.4 jit_solution(17229548271596959876)
XLA Ops:
  7.2 0.0 copy-start
  7.2 1.8 copy-done
  8.9 5.4 %multiply_reduce_fusion.1 = (f32[384]{0:T(512)S(1)}, f32[384,1024]{1,0:T(8,128)S(1)}) fusion(bf16[384,3584]{1,0:T(8,128)(2,1)S(1)} %copy-done, bf16[3584,1024]{1,0:T(8,128)(2,1)} %param.6), kind=kOutput, calls=%fused_computation.22 | convolution fusion | flops 2819358208 | bytes 11666944 | tf_op jit(solution)/shard_map/dot_general | solution.py:21
  14.3 0.0 copy-start.2
  14.4 1.2 copy-done.2
  15.5 0.2 fusion.22
  15.8 6.1 %stack.2 = bf16[16,384,1024]{2,1,0:T(8,128)(2,1)} broadcast(bf16[384,1024]{1,0:T(8,128)(2,1)S(1)} %fusion.22), dimensions={1,2} | broadcast | bytes 13369344 | tf_op jit(solution)/shard_map/stack | solution.py:10
  21.9 0.0 copy-start.10
  21.9 0.0 copy-start.9
  21.9 8.6 %all-to-all-start = ((bf16[16,384,1024]{2,1,0:T(8,128)(2,1)}), bf16[16,384,1024]{2,1,0:T(8,128)(2,1)}, u32[]{:S(2)}, u32[]{:S(2)}) async-start(bf16[16,384,1024]{2,1,0:T(8,128)(2,1)} %stack.2), calls=%async_computation | async-start | bytes 25165824 | tf_op jit(solution)/shard_map/all_to_all | solution.py:11
  30.5 0.0 all-reduce.3.cloned.1.call-start
  31.2 0.0 copy-done.10
  31.2 0.1 fusion.18
  31.3 0.7 iota_compare_fusion.1
  32.0 0.0 copy-done.9
  32.0 0.8 iota_compare_fusion
  32.8 183.7 %all-to-all-done = bf16[16,384,1024]{2,1,0:T(8,128)(2,1)} async-done(((bf16[16,384,1024]{2,1,0:T(8,128)(2,1)}), bf16[16,384,1024]{2,1,0:T(8,128)(2,1)}, u32[]{:S(2)}, u32[]{:S(2)}) %all-to-all-start) | async-done | bytes 12582944 | tf_op jit(solution)/shard_map/all_to_all | solution.py:11
  216.4 10.3 %gather_fusion = bf16[13,384,1024]{2,1,0:T(8,128)(2,1)} fusion(bf16[16,384,1024]{2,1,0:T(8,128)(2,1)} %all-to-all-done, s32[1024]{0:T(1024)S(1)} %pad_clamp_fusion), kind=kCustom, calls=%fused_computation | custom fusion | bytes 20447284 | tf_op jit(solution)/shard_map/gather | solution.py:27
  226.7 0.0 copy-start.5
  226.7 0.0 copy-start.7
  226.7 9.9 %fusion.11 = (f32[384]{0:T(512)S(1)}, f32[13,384,384]{2,1,0:T(8,128)S(1)}) fusion(f32[]{:T(128)} %bitcast.43, pred[384,384]{0,1:T(8,128)(4,1)} %iota_compare_fusion.1, pred[13]{0:T(512)(128)(4,1)S(1)} %iota_compare_fusion.2, bf16[13,384,1024]{2,1,0:T(8,128)(2,1)} %gather_fusion, bf16[384,1024]{1,0:T(8,128)(2,1)S(1)} %fusion.22), kind=kOutput, calls=%fused_computation.18 | convolution fusion | flops 3933535744 | bytes 18826768 | tf_op jit(solution)/shard_map/id,pjd->pij/dot_general | solution.py:33
  236.7 0.0 copy-start.1
  236.7 0.0 copy-start.6
  236.7 0.0 copy-start.8
  236.7 3.0 copy-done.1
  239.7 0.0 copy-done.5
  239.7 0.0 copy-done.7
  239.7 3.2 fusion
  242.9 0.6 subtract_reduce_fusion
  243.5 16.3 %all-gather = f32[16,1,384]{2,1,0:T(1,128)S(1)} all-gather(f32[1,1,384]{2,1,0:T(1,128)S(1)} %reshape.159), channel_id=1, replica_groups=mesh['group'=8,'member'=16] {'member'}, dimensions={0}, use_global_device_ids=true | all-gather | bytes 26112 | tf_op jit(solution)/shard_map/all_gather | solution.py:42
  259.8 0.6 gather_fusion.1
  260.3 0.0 copy-done.6
  260.4 0.0 copy-done.8
  260.4 0.0 copy-start.3
  260.4 12.8 %multiply_reduce_fusion = (f32[384]{0:T(512)S(1)}, f32[384,1024]{1,0:T(8,128)S(1)}) fusion(f32[384,1024]{1,0:T(8,128)} %copy-done.2, f32[384]{0:T(512)S(1)} %add_sqrt_fusion, bf16[13,384,1024]{2,1,0:T(8,128)(2,1)} %gather_fusion, f32[13,384]{1,0:T(8,128)S(1)} %gather_fusion.1, f32[384]{0:T(512)S(1)} %get-tuple-element.12, ...), kind=kOutput, calls=%fused_computation.21 | convolution fusion | flops 3946610176 | bytes 21356560 | tf_op jit(solution)/shard_map/pij,pjd->id/dot_general | solution.py:46
  273.1 0.0 copy-start.4
  273.1 1.1 copy-done.4
  274.3 0.0 copy-done.3
  274.3 7.5 %convolution_bitcast_fusion = f32[3584,1024]{0,1:T(8,128)} fusion(bf16[384,3584]{1,0:T(8,128)(2,1)S(1)} %copy-done, f32[384,1024]{1,0:T(8,128)S(1)} %get-tuple-element.18, f32[384]{0:T(512)S(1)} %get-tuple-element.17, f32[384]{0:T(512)S(1)} %add_sqrt_fusion, f32[384,1024]{1,0:T(8,128)S(1)} %copy-done.3), kind=kOutput, calls=%fused_computation.4 | convolution fusion | flops 2820538368 | bytes 20581376 | tf_op jit(solution)/shard_map/dot_general | solution.py:55
  281.8 0.0 all-reduce.3.cloned.1.call-update
  281.9 71.4 %psum.7 = f32[]{:T(128)} all-reduce(f32[]{:T(128)} %get-tuple-element.11), channel_id=1, replica_groups=mesh['group'=8,'member'=16] {'group','member'}, use_global_device_ids=true, to_apply=%region_5.6 | all-reduce | flops 1 | bytes 8 | tf_op jit(solution)/shard_map/psum | solution.py:40
  353.9 8.8 %convolution_convert_fusion = bf16[384,3584]{1,0:T(8,128)(2,1)} fusion(bf16[3584,1024]{1,0:T(8,128)(2,1)} %param.6, f32[384,1024]{1,0:T(8,128)} %copy-done.4, f32[384]{0:T(512)S(1)} %get-tuple-element.17, f32[384]{0:T(512)S(1)} %add_sqrt_fusion, f32[384,1024]{1,0:T(8,128)} %copy-done.2), kind=kOutput, calls=%fused_computation.10 | convolution fusion | flops 2821914624 | bytes 13241344 | tf_op jit(solution)/shard_map/dot_general | solution.py:51
  362.7 98.4 %all-reduce.3.cloned.1.call-done = f32[3584,1024]{0,1:T(8,128)} async-done(((f32[3584,1024]{0,1:T(8,128)}), f32[3584,1024]{0,1:T(8,128)}) %all-reduce.3.cloned.1.call-update) | async-done | bytes 14680080
  461.2 1.4 constant_dynamic-slice_fusion
  462.6 0.9 copy.11
  (7 shorter events, 0.0 us)
Async XLA Ops:
  7.2 1.8 copy-start
  14.3 1.2 copy-start.2
  21.9 9.3 %copy-start.10 = (s32[1,12]{1,0:T(1,128)S(1)}, s32[1,12]{1,0:T(1,128)}, u32[]{:S(2)}) copy-start(s32[1,12]{1,0:T(1,128)} %param.8) | copy-start | bytes 148
  21.9 10.2 %copy-start.9 = (s32[384]{0:T(512)S(1)}, s32[384]{0:T(512)}, u32[]{:S(2)}) copy-start(s32[384]{0:T(512)} %param.9) | copy-start | bytes 4612
  21.9 194.6 %all-to-all-start = ((bf16[16,384,1024]{2,1,0:T(8,128)(2,1)}), bf16[16,384,1024]{2,1,0:T(8,128)(2,1)}, u32[]{:S(2)}, u32[]{:S(2)}) async-start(bf16[16,384,1024]{2,1,0:T(8,128)(2,1)} %stack.2), calls=%async_computation | async-start | bytes 25165824 | tf_op jit(solution)/shard_map/all_to_all | solution.py:11
  30.5 430.7 %all-reduce.3.cloned.1.call-start = ((), (), s32[]{:S(2)}) async-start(), calls=%async_computation.1 | async-start | bytes 29360128
  226.7 13.0 %copy-start.5 = (pred[384,384]{0,1:T(8,128)(4,1)S(1)}, pred[384,384]{0,1:T(8,128)(4,1)}, u32[]{:S(2)}) copy-start(pred[384,384]{0,1:T(8,128)(4,1)} %iota_compare_fusion.1) | copy-start | bytes 442372
  226.7 13.0 %copy-start.7 = (pred[384,384]{0,1:T(8,128)(4,1)S(1)}, pred[384,384]{0,1:T(8,128)(4,1)}, u32[]{:S(2)}) copy-start(pred[384,384]{0,1:T(8,128)(4,1)} %iota_compare_fusion) | copy-start | bytes 442372
  236.7 3.0 copy-start.1
  236.7 23.7 %copy-start.6 = (pred[384,384]{0,1:T(8,128)(4,1)S(1)}, pred[384,384]{0,1:T(8,128)(4,1)}, u32[]{:S(2)}) copy-start(pred[384,384]{0,1:T(8,128)(4,1)} %iota_compare_fusion.1) | copy-start | bytes 442372
  236.7 23.7 %copy-start.8 = (pred[384,384]{0,1:T(8,128)(4,1)S(1)}, pred[384,384]{0,1:T(8,128)(4,1)}, u32[]{:S(2)}) copy-start(pred[384,384]{0,1:T(8,128)(4,1)} %iota_compare_fusion) | copy-start | bytes 442372
  260.4 13.9 %copy-start.3 = (f32[384,1024]{1,0:T(8,128)S(1)}, f32[384,1024]{1,0:T(8,128)}, u32[]{:S(2)}) copy-start(f32[384,1024]{1,0:T(8,128)} %copy-done.2) | copy-start | bytes 4718596
  273.1 1.1 copy-start.4
Sparse Core Ops, SparseCore 0:
  282.0 179.1 all-reduce.2
